TPU v7x, 512 devices: a whole 4x4x16 slice. The times are simulated.
512 devices in a mesh: lev: 32 (over x_lo, z), mem: 16 (over x_hi, y, core).
Axes of the slice: x: 4 (x_hi: 2, x_lo: 2; x = x_hi * 2 + x_lo), y: 4, z: 16, core: 2. Of those that a mesh axis runs over, the one named last changes fastest.
Arguments:
- control: bfloat16 [32, 5, 128, 4096], P('mem', None, 'lev'), may hold values from -6 to 6
- static_control_vector: bfloat16 [5, 128, 4096], P(None, None, 'lev'), may hold values from -6 to 6
- perturb: bfloat16 [32, 5, 128, 4096], P('mem', None, None, 'lev'), may hold values from -6 to 6
- tiles: bfloat16 [4, 64, 64], replicated, may hold values from -0.375 to 0.375
- block_offset: int32 [64, 4], replicated, may hold values from -8 to 8
- vert: bfloat16 [5, 128, 128], replicated, may hold values from -0.5 to 0.5
- static_vertical_root: bfloat16 [5, 128, 128], replicated, may hold values from -0.5 to 0.5
- obs_index: int32 [524288], P(('lev', 'mem')), may hold values from 0 to 5119
- obs_value: float32 [524288], P(('lev', 'mem')), may hold values from -6 to 6
- obs_sigma: float32 [524288], P(('lev', 'mem')), may hold values from 0.3 to 1
- huber_mask: int32 [524288], P(('lev', 'mem')), may hold values 0 or 1
Outputs:
- control_out: bfloat16 [32, 5, 128, 4096], P('mem', None, 'lev')
- static_out: bfloat16 [5, 128, 4096], P(None, None, 'lev')
Inputs may be any that keep to these rules, and one draw needn't show every extreme that they name: `obs_index`: indices count in the block held by the observation's own device: 5 variables, 128 / 16 levels, 128 columns, in that order. `block_offset`: source blocks wrap around the window.
All inputs are finite; a program needn't handle non-finite values. No bound on the sum of `huber_mask` on one device may be relied on, other than what follows from the above.
Results may differ from a plain program's by a relative error of at most 0.0057.
Values may be sent and summed in bfloat16 or wider, within the bound.
No kernel may reach another device: no remote copies, remote signals or barrier semaphores. Data moves between devices by JAX's collectives and lax.ppermute only.
A program may use at most 64 MiB of HBM per device.

v0:
```python
import math
import jax
import jax.numpy as jnp
from jax import lax
from jax.sharding import PartitionSpec as P

ITERS = 2
ENS_W = 0.85
STATIC_WEIGHT = 0.5
TAU = 0.5
HUBER_LOW = 0.3


def selectors(block_offset):
    count = block_offset.shape[0]
    blocks = jnp.arange(count, dtype=jnp.int32)
    source = (blocks[:, None] + block_offset) % count
    return (source.T[:, :, None] == blocks[None, None, :]).astype(jnp.bfloat16)


def horizontal(field, tiles, picks):
    count = picks.shape[1]
    width = tiles.shape[1]
    shaped = field.reshape(field.shape[:-1] + (count, width))
    total = None
    for slot in range(tiles.shape[0]):
        moved = jnp.einsum(
            "bj,...jc->...bc", picks[slot], shaped, preferred_element_type=jnp.float32
        ).astype(jnp.bfloat16)
        term = jnp.einsum("...bc,cd->...bd", moved, tiles[slot], preferred_element_type=jnp.float32)
        total = term if total is None else total + term
    return total.reshape(field.shape).astype(jnp.bfloat16)


def horizontal_adjoint(field, tiles, picks):
    count = picks.shape[1]
    width = tiles.shape[1]
    shaped = field.reshape(field.shape[:-1] + (count, width))
    total = None
    for slot in range(tiles.shape[0]):
        term = jnp.einsum(
            "...bc,dc->...bd", shaped, tiles[slot], preferred_element_type=jnp.float32
        )
        moved = jnp.einsum(
            "bj,...bd->...jd",
            picks[slot].astype(jnp.float32),
            term,
            precision=lax.Precision.HIGHEST,
        )
        total = moved if total is None else total + moved
    return total.reshape(field.shape)


def observe(block, obs_index, obs_value, precision_obs):
    flat = block.reshape(-1)
    seen = flat[obs_index]
    resid = precision_obs * (seen - obs_value)
    return jnp.zeros_like(flat).at[obs_index].add(resid).reshape(block.shape)


def on_device(
    control,
    static_control_vector,
    perturb,
    tiles,
    block_offset,
    vert,
    static_vertical_root,
    obs_index,
    obs_value,
    obs_sigma,
    huber_mask,
):
    picks = selectors(block_offset)
    members_all = control.shape[0] * lax.axis_size("mem")
    ens_gain = ENS_W / math.sqrt(members_all)
    level_rows = static_control_vector.shape[1] // lax.axis_size("mem")
    first_level = lax.axis_index("mem") * level_rows
    weights = jnp.where(huber_mask == 1, jnp.float32(1.0), jnp.float32(HUBER_LOW))
    precision_obs = weights / (obs_sigma * obs_sigma)
    vertical_forward = vert.astype(jnp.float32)
    static_forward = static_vertical_root.astype(jnp.float32)
    for turn in range(ITERS):
        local = horizontal(control, tiles, picks)
        columns = lax.all_to_all(local, "lev", split_axis=3, concat_axis=2, tiled=True)
        vertical = jnp.einsum("vlk,mvkc->mvlc", vert, columns, preferred_element_type=jnp.float32)
        partial_value = jnp.sum(vertical * perturb.astype(jnp.float32), axis=0)
        static_portion = jnp.einsum(
            "tbu,tuo->tbo",
            static_vertical_root,
            static_control_vector,
            preferred_element_type=jnp.float32,
        )
        ens = lax.psum(partial_value, "mem")
        increment = ens_gain * ens + STATIC_WEIGHT * static_portion
        own_block = lax.dynamic_slice_in_dim(increment, first_level, level_rows, 1)
        grad_block = observe(own_block, obs_index, obs_value, precision_obs)
        placed = lax.dynamic_update_slice_in_dim(
            jnp.zeros_like(increment), grad_block, first_level, 1
        )
        gradient_field_total = lax.psum(placed, "mem")
        static_gradient = static_control_vector.astype(jnp.float32) + STATIC_WEIGHT * jnp.einsum(
            "otn,ote->one", static_forward, gradient_field_total, precision=lax.Precision.HIGHEST
        )
        weighted_innovations = (ens_gain * gradient_field_total)[None] * perturb.astype(jnp.float32)
        backward_field = jnp.einsum(
            "vkl,mvkc->mvlc",
            vertical_forward,
            weighted_innovations,
            precision=lax.Precision.HIGHEST,
        ).astype(jnp.bfloat16)
        levels = lax.all_to_all(backward_field, "lev", split_axis=2, concat_axis=3, tiled=True)
        adjoint = horizontal_adjoint(levels, tiles, picks)
        current = control.astype(jnp.float32)
        control = (current - TAU * (current + adjoint)).astype(jnp.bfloat16)
        static_control_vector = (
            static_control_vector.astype(jnp.float32) - TAU * static_gradient
        ).astype(jnp.bfloat16)
    return (control, static_control_vector)


def solution(mesh):
    placed = (
        P("mem", None, "lev", None),
        P(None, None, "lev"),
        P("mem", None, None, "lev"),
        P(),
        P(),
        P(),
        P(),
        P(("lev", "mem")),
        P(("lev", "mem")),
        P(("lev", "mem")),
        P(("lev", "mem")),
    )
    return jax.shard_map(
        on_device,
        mesh=mesh,
        in_specs=placed,
        out_specs=(P("mem", None, "lev", None), P(None, None, "lev")),
        check_vma=False,
    )
```

profile of v0, /device:TPU:4, one launch (start us, length us, event | category | flops | bytes accessed | tf_op | source)
XLA Modules:
  0.0 919.5 jit_solution(7885680321525011483)
XLA Ops:
  8.0 1.6 reshape.43
  9.6 1.2 fusion.5
  12.5 9.9 %copy.161 = bf16[2,5,4,64,64]{1,2,0,4,3:T(4,128)(2,1)} copy(bf16[2,5,4,64,64]{4,3,2,1,0:T(8,128)(2,1)S(1)} %fusion.2) | data formatting | bytes 655360 | tf_op jit(solution)/shard_map/convert_element_type | solution.py:32
  22.3 13.3 %reshape.102 = bf16[32,2,2560]{2,1,0:T(2,128)(2,1)} reshape(bf16[4096,2,4,5]{3,2,1,0:T(4,128)(2,1)} %bitcast.255) | data formatting | bytes 655360
  35.6 16.1 %all-to-all-start = ((bf16[32,2,2560]{2,1,0:T(2,128)(2,1)}), bf16[32,2,2560]{2,1,0:T(2,128)(2,1)S(1)}, u32[]{:S(2)}, u32[]{:S(2)}) async-start(bf16[32,2,2560]{2,1,0:T(2,128)(2,1)} %reshape.102), calls=%async_computation | async-start | bytes 655360 | tf_op jit(solution)/shard_map/all_to_all | solution.py:85
  52.0 24.5 %all-to-all-done = bf16[32,2,2560]{2,1,0:T(2,128)(2,1)S(1)} async-done(((bf16[32,2,2560]{2,1,0:T(2,128)(2,1)}), bf16[32,2,2560]{2,1,0:T(2,128)(2,1)S(1)}, u32[]{:S(2)}, u32[]{:S(2)}) %all-to-all-start) | async-done | bytes 327712 | tf_op jit(solution)/shard_map/all_to_all | solution.py:85
  76.5 19.2 %reshape.103 = bf16[4096,2,4,5]{3,2,1,0:T(4,128)(2,1)} reshape(bf16[32,2,2560]{2,1,0:T(2,128)(2,1)S(1)} %all-to-all-done) | data formatting | bytes 655360
  95.7 11.4 %copy.89 = bf16[2,5,4,32,128]{4,2,3,1,0:T(4,128)(2,1)S(1)} copy(bf16[2,5,4,32,128]{1,2,0,4,3:T(4,128)(2,1)} %bitcast.256) | data formatting | bytes 655360 | tf_op jit(solution)/shard_map/all_to_all | solution.py:85
  108.7 143.3 %all-reduce.5.cloned.1.call-done = f32[5,128,128]{2,1,0:T(8,128)} async-done(((f32[5,128,128]{2,1,0:T(8,128)}), f32[5,128,128]{2,1,0:T(8,128)}) %all-reduce.5.cloned.1.call-update) | async-done | bytes 327696 | tf_op jit(solution)/shard_map/psum | solution.py:94
  252.7 6.2 gather_fusion
  258.9 5.9 scatter_custom_fusion
  265.7 151.5 %all-reduce.7.cloned.1.call-done = f32[5,128,128]{2,1,0:T(8,128)} async-done(((f32[5,128,128]{2,1,0:T(8,128)}), f32[5,128,128]{2,1,0:T(8,128)}) %all-reduce.7.cloned.1.call-update) | async-done | bytes 327696 | tf_op jit(solution)/shard_map/psum | solution.py:101
  417.2 1.0 broadcast_multiply_fusion
  419.6 36.8 %all_to_all.66 = bf16[2,5,128,128]{3,0,1,2:T(2,128)(2,1)S(1)} all-to-all(bf16[2,5,128,128]{3,0,1,2:T(2,128)(2,1)S(1)} %copy.95), channel_id=1, replica_groups=mesh['lev'=32,'mem'=16] {'lev'}, dimensions={2} | all-to-all | bytes 655360 | tf_op jit(solution)/shard_map/all_to_all | solution.py:112
  462.1 1.8 fusion.1
  463.9 1.7 copy.102
  468.1 1.8 convolution_add_fusion.2
  469.8 2.0 convolution_add_fusion.1
  471.9 1.6 fusion.3
  473.4 11.7 %copy.163 = bf16[2,5,4,64,64]{1,2,0,4,3:T(4,128)(2,1)} copy(bf16[2,5,4,64,64]{4,3,2,1,0:T(8,128)(2,1)} %fusion.3) | data formatting | bytes 655360 | tf_op jit(solution)/shard_map/convert_element_type | solution.py:32
  485.1 13.2 %reshape.104 = bf16[32,2,2560]{2,1,0:T(2,128)(2,1)} reshape(bf16[4096,2,4,5]{3,2,1,0:T(4,128)(2,1)} %bitcast.257) | data formatting | bytes 655360
  498.3 3.9 all-to-all-start.2
  502.7 21.9 %all-to-all-done.2 = bf16[32,2,2560]{2,1,0:T(2,128)(2,1)S(1)} async-done(((bf16[32,2,2560]{2,1,0:T(2,128)(2,1)}), bf16[32,2,2560]{2,1,0:T(2,128)(2,1)S(1)}, u32[]{:S(2)}, u32[]{:S(2)}) %all-to-all-start.2) | async-done | bytes 327712 | tf_op jit(solution)/shard_map/all_to_all | solution.py:85
  524.5 19.2 %reshape.105 = bf16[4096,2,4,5]{3,2,1,0:T(4,128)(2,1)} reshape(bf16[32,2,2560]{2,1,0:T(2,128)(2,1)S(1)} %all-to-all-done.2) | data formatting | bytes 655360
  543.7 11.4 %copy.112 = bf16[2,5,4,32,128]{4,2,3,1,0:T(4,128)(2,1)S(1)} copy(bf16[2,5,4,32,128]{1,2,0,4,3:T(4,128)(2,1)} %bitcast.258) | data formatting | bytes 655360 | tf_op jit(solution)/shard_map/all_to_all | solution.py:85
  557.1 142.3 %all-reduce.9.cloned.1.call-done = f32[5,128,128]{2,1,0:T(8,128)} async-done(((f32[5,128,128]{2,1,0:T(8,128)}), f32[5,128,128]{2,1,0:T(8,128)}) %all-reduce.9.cloned.1.call-update) | async-done | bytes 327696 | tf_op jit(solution)/shard_map/psum | solution.py:94
  700.2 6.1 gather_fusion.1
  706.3 6.1 scatter_custom_fusion.1
  713.2 151.5 %all-reduce.11.cloned.1.call-done = f32[5,128,128]{2,1,0:T(8,128)} async-done(((f32[5,128,128]{2,1,0:T(8,128)}), f32[5,128,128]{2,1,0:T(8,128)}) %all-reduce.11.cloned.1.call-update) | async-done | bytes 327696 | tf_op jit(solution)/shard_map/psum | solution.py:101
  866.4 1.3 copy.120
  867.6 13.5 %all-to-all-start.3 = ((bf16[2,5,128,128]{3,0,1,2:T(2,128)(2,1)}), bf16[2,5,128,128]{3,0,1,2:T(2,128)(2,1)S(1)}, u32[]{:S(2)}, u32[]{:S(2)}) async-start(bf16[2,5,128,128]{3,0,1,2:T(2,128)(2,1)} %copy.120), calls=%async_computation.3 | async-start | bytes 655360 | tf_op jit(solution)/shard_map/all_to_all | solution.py:112
  882.4 22.2 %all-to-all-done.3 = bf16[2,5,128,128]{3,0,1,2:T(2,128)(2,1)S(1)} async-done(((bf16[2,5,128,128]{3,0,1,2:T(2,128)(2,1)}), bf16[2,5,128,128]{3,0,1,2:T(2,128)(2,1)S(1)}, u32[]{:S(2)}, u32[]{:S(2)}) %all-to-all-start.3) | async-done | bytes 327712 | tf_op jit(solution)/shard_map/all_to_all | solution.py:112
  (97 shorter events, 30.1 us)
Async XLA Ops:
  7.2 100.0 %copy-start = (bf16[5,128,128]{2,1,0:T(8,128)(2,1)S(1)}, bf16[5,128,128]{2,1,0:T(8,128)(2,1)}, u32[]{:S(2)}) copy-start(bf16[5,128,128]{2,1,0:T(8,128)(2,1)} %param.16) | copy-start | bytes 491524
  8.0 2.8 copy-start.7
  22.3 29.4 %copy-start.9 = (bf16[2,5,128,128]{3,2,1,0:T(8,128)(2,1)S(1)}, bf16[2,5,128,128]{3,2,1,0:T(8,128)(2,1)}, u32[]{:S(2)}) copy-start(bf16[2,5,128,128]{3,2,1,0:T(8,128)(2,1)} %param.13) | copy-start | bytes 983044
  35.6 40.9 %all-to-all-start = ((bf16[32,2,2560]{2,1,0:T(2,128)(2,1)}), bf16[32,2,2560]{2,1,0:T(2,128)(2,1)S(1)}, u32[]{:S(2)}, u32[]{:S(2)}) async-start(bf16[32,2,2560]{2,1,0:T(2,128)(2,1)} %reshape.102), calls=%async_computation | async-start | bytes 655360 | tf_op jit(solution)/shard_map/all_to_all | solution.py:85
  51.7 200.2 %all-reduce.5.cloned.1.call-start = ((), (), s32[]{:S(2)}) async-start(), calls=%async_computation.4 | async-start | bytes 655360 | tf_op jit(solution)/shard_map/psum | solution.py:94
  107.1 1.3 copy-start.13
  107.1 1.4 copy-start.1
  107.1 1.4 copy-start.8
  108.4 308.8 %all-reduce.7.cloned.1.call-start = ((), (), s32[]{:S(2)}) async-start(), calls=%async_computation.5 | async-start | bytes 655360 | tf_op jit(solution)/shard_map/psum | solution.py:101
  108.5 150.5 %copy-start.14 = (s32[1024]{0:T(1024)}, s32[1024]{0:T(1024)S(1)}, u32[]{:S(2)}) copy-start(s32[1024]{0:T(1024)S(1)} %get-tuple-element.11) | copy-start | bytes 12292
  252.7 6.2 copy-start.10
  252.7 6.2 copy-start.11
  252.7 6.2 copy-start.12
  264.9 0.7 copy-start.6
  465.6 1.0 copy-start.4
  498.3 26.2 %all-to-all-start.2 = ((bf16[32,2,2560]{2,1,0:T(2,128)(2,1)}), bf16[32,2,2560]{2,1,0:T(2,128)(2,1)S(1)}, u32[]{:S(2)}, u32[]{:S(2)}) async-start(bf16[32,2,2560]{2,1,0:T(2,128)(2,1)} %reshape.104), calls=%async_computation.2 | async-start | bytes 655360 | tf_op jit(solution)/shard_map/all_to_all | solution.py:85
  502.2 197.2 %all-reduce.9.cloned.1.call-start = ((), (), s32[]{:S(2)}) async-start(), calls=%async_computation.6 | async-start | bytes 655360 | tf_op jit(solution)/shard_map/psum | solution.py:94
  555.1 1.3 copy-start.2
  556.4 308.4 %all-reduce.11.cloned.1.call-start = ((), (), s32[]{:S(2)}) async-start(), calls=%async_computation.7 | async-start | bytes 655360 | tf_op jit(solution)/shard_map/psum | solution.py:101
  712.5 0.7 copy-start.5
  865.9 15.2 %copy-start.3 = (f32[5,128,128]{2,1,0:T(8,128)S(1)}, f32[5,128,128]{2,1,0:T(8,128)}, u32[]{:S(2)}) copy-start(f32[5,128,128]{2,1,0:T(8,128)} %all-reduce.11.cloned.1.call-done) | copy-start | bytes 983044
  867.6 37.0 %all-to-all-start.3 = ((bf16[2,5,128,128]{3,0,1,2:T(2,128)(2,1)}), bf16[2,5,128,128]{3,0,1,2:T(2,128)(2,1)S(1)}, u32[]{:S(2)}, u32[]{:S(2)}) async-start(bf16[2,5,128,128]{3,0,1,2:T(2,128)(2,1)} %copy.120), calls=%async_computation.3 | async-start | bytes 655360 | tf_op jit(solution)/shard_map/all_to_all | solution.py:112
Sparse Core Ops, SparseCore 0:
  108.5 143.3 all-reduce.4
  265.8 151.3 all-reduce.6
  556.5 142.9 all-reduce.8
  713.3 151.3 all-reduce.10
where the time goes:
time: 922 us; the launch traced here: 920 us
  waiting for transfers between devices  657 us (71%)
  local copies, waits for them, and re-layouts  135 us (15%)
  blocking collectives  36.8 us (4%)
  starting transfers between devices  33.9 us (4%)
  matrix products  24.7 us (3%)
  other arithmetic  17.5 us (2%)
  between operations  14.4 us (2%)
    psum x2, waiting for transfers between devices, on_device(): gradient_field_total = lax.psum(placed, 'mem')  303 us
    psum x2, waiting for transfers between devices, on_device(): ens = lax.psum(partial_value, 'mem')  286 us
    unnamed x37, local copies, waits for them, and re-layouts  67.9 us
    all_to_all x2, waiting for transfers between devices, on_device(): lax.all_to_all(local, 'lev', split_axis=3, concat_axis=2, tiled=True)  46.4 us
    all_to_all x1, blocking collectives, on_device(): lax.all_to_all(backward_field, 'lev', split_axis=2, concat_axis=3, tiled=...  36.8 us
    all_to_all x2, local copies, waits for them, and re-layouts, on_device(): lax.all_to_all(local, 'lev', split_axis=3, concat_axis=2, tiled=True)  22.9 us
    all_to_all x1, waiting for transfers between devices, on_device(): lax.all_to_all(backward_field, 'lev', split_axis=2, concat_axis=3, tiled=...  22.2 us
    convert_element_type x2, local copies, waits for them, and re-layouts, horizontal(): return total.reshape(field.shape).astype(jnp.bfloat16)  21.5 us
  transfers between devices with their start and end apart: 7, of which 7 were waited for; matrix products, arithmetic and copies ran while one was open for 0% of the time, Pallas kernels for 0%

commit v1 on v0

--- a/solution.py
+++ b/solution.py
@@ -82,7 +82,10 @@
     static_forward = static_vertical_root.astype(jnp.float32)
     for turn in range(ITERS):
         local = horizontal(control, tiles, picks)
-        columns = lax.all_to_all(local, "lev", split_axis=3, concat_axis=2, tiled=True)
+        columns = jnp.concatenate(
+            lax.all_to_all(jnp.stack(jnp.split(local, lax.axis_size("lev"), axis=3)), "lev", 0, 0),
+            axis=2,
+        )
         vertical = jnp.einsum("vlk,mvkc->mvlc", vert, columns, preferred_element_type=jnp.float32)
         partial_value = jnp.sum(vertical * perturb.astype(jnp.float32), axis=0)
         static_portion = jnp.einsum(

time: 922 us -> 852 us (0.924)
  local copies, waits for them, and re-layouts: 135 us -> 66.8 us
    unnamed x37 -> x95, local copies, waits for them, and re-layouts: 67.9 us -> 40.7 us
    all_to_all x2 -> x0, local copies, waits for them, and re-layouts: 22.9 us -> none  [on_device(): lax.all_to_all(local, 'lev', split_axis=3, concat_axis=2, tiled=True)]
    convert_element_type x2, local copies, waits for them, and re-layouts: 21.5 us -> 2 us  [horizontal(): return total.reshape(field.shape).astype(jnp.bfloat16)]
where the time goes in v1:
time: 852 us; the launch traced here: 851 us
  waiting for transfers between devices  657 us (77%)
  local copies, waits for them, and re-layouts  66.8 us (8%)
  blocking collectives  36.8 us (4%)
  starting transfers between devices  33.9 us (4%)
  matrix products  24.7 us (3%)
  other arithmetic  17.5 us (2%)
  between operations  14.4 us (2%)
    psum x2, waiting for transfers between devices, on_device(): gradient_field_total = lax.psum(placed, 'mem')  303 us
    psum x2, waiting for transfers between devices, on_device(): ens = lax.psum(partial_value, 'mem')  285 us
    all_to_all x2, waiting for transfers between devices, on_device(): lax.all_to_all(jnp.stack(jnp.split(local, lax.axis_size('lev'), axis=3)),...  46.6 us
    unnamed x95, local copies, waits for them, and re-layouts  40.7 us
    all_to_all x1, blocking collectives, on_device(): lax.all_to_all(backward_field, 'lev', split_axis=2, concat_axis=3, tiled=...  36.8 us
    all_to_all x1, waiting for transfers between devices, on_device(): lax.all_to_all(backward_field, 'lev', split_axis=2, concat_axis=3, tiled=...  22.2 us
    all_to_all x2, starting transfers between devices, on_device(): lax.all_to_all(jnp.stack(jnp.split(local, lax.axis_size('lev'), axis=3)),...  20 us
  transfers between devices with their start and end apart: 7, of which 7 were waited for; matrix products, arithmetic and copies ran while one was open for 0% of the time, Pallas kernels for 0%

profile of v1, /device:TPU:4, one launch (start us, length us, event | category | flops | bytes accessed | tf_op | source)
XLA Modules:
  0.0 851.3 jit_solution(6151782144119729264)
XLA Ops:
  8.0 1.6 reshape.55
  9.6 1.2 fusion.5
  32.4 16.1 %all-to-all-start = ((bf16[32,2,5,4,128]{4,3,2,1,0:T(4,128)(2,1)}), bf16[32,2,5,4,128]{4,3,2,1,0:T(4,128)(2,1)S(1)}, u32[]{:S(2)}, u32[]{:S(2)}) async-start(bf16[32,2,5,4,128]{4,3,2,1,0:T(4,128)(2,1)} %constant_dynamic-update-slice_fusion), calls=%async_computation | async-start | bytes 655360 | tf_op jit(solution)/shard_map/all_to_all | solution.py:86
  48.7 24.5 %all-to-all-done = bf16[32,2,5,4,128]{4,3,2,1,0:T(4,128)(2,1)S(1)} async-done(((bf16[32,2,5,4,128]{4,3,2,1,0:T(4,128)(2,1)}), bf16[32,2,5,4,128]{4,3,2,1,0:T(4,128)(2,1)S(1)}, u32[]{:S(2)}, u32[]{:S(2)}) %all-to-all-start) | async-done | bytes 327712 | tf_op jit(solution)/shard_map/all_to_all | solution.py:86
  73.7 0.9 copy.110
  75.0 143.2 %all-reduce.5.cloned.1.call-done = f32[5,128,128]{2,1,0:T(8,128)} async-done(((f32[5,128,128]{2,1,0:T(8,128)}), f32[5,128,128]{2,1,0:T(8,128)}) %all-reduce.5.cloned.1.call-update) | async-done | bytes 327696 | tf_op jit(solution)/shard_map/psum | solution.py:97
  218.9 6.2 gather_fusion
  225.1 5.9 scatter_custom_fusion
  231.9 151.5 %all-reduce.7.cloned.1.call-done = f32[5,128,128]{2,1,0:T(8,128)} async-done(((f32[5,128,128]{2,1,0:T(8,128)}), f32[5,128,128]{2,1,0:T(8,128)}) %all-reduce.7.cloned.1.call-update) | async-done | bytes 327696 | tf_op jit(solution)/shard_map/psum | solution.py:104
  383.4 1.0 broadcast_multiply_fusion
  385.0 0.8 copy.113
  385.8 36.8 %all_to_all.40 = bf16[2,5,128,128]{3,0,1,2:T(2,128)(2,1)S(1)} all-to-all(bf16[2,5,128,128]{3,0,1,2:T(2,128)(2,1)S(1)} %copy.113), channel_id=1, replica_groups=mesh['lev'=32,'mem'=16] {'lev'}, dimensions={2} | all-to-all | bytes 655360 | tf_op jit(solution)/shard_map/all_to_all | solution.py:115
  428.3 1.8 fusion.1
  430.1 1.7 copy.120
  434.3 1.8 convolution_add_fusion.2
  436.1 2.0 convolution_add_fusion.1
  438.1 1.5 fusion.3
  439.6 1.5 convert_element_type.140
  460.6 3.9 all-to-all-start.2
  464.7 22.1 %all-to-all-done.2 = bf16[32,2,5,4,128]{4,3,2,1,0:T(4,128)(2,1)S(1)} async-done(((bf16[32,2,5,4,128]{4,3,2,1,0:T(4,128)(2,1)}), bf16[32,2,5,4,128]{4,3,2,1,0:T(4,128)(2,1)S(1)}, u32[]{:S(2)}, u32[]{:S(2)}) %all-to-all-start.2) | async-done | bytes 327712 | tf_op jit(solution)/shard_map/all_to_all | solution.py:86
  487.2 0.9 copy.131
  489.1 142.1 %all-reduce.9.cloned.1.call-done = f32[5,128,128]{2,1,0:T(8,128)} async-done(((f32[5,128,128]{2,1,0:T(8,128)}), f32[5,128,128]{2,1,0:T(8,128)}) %all-reduce.9.cloned.1.call-update) | async-done | bytes 327696 | tf_op jit(solution)/shard_map/psum | solution.py:97
  632.0 6.1 gather_fusion.1
  638.1 6.1 scatter_custom_fusion.1
  645.0 151.5 %all-reduce.11.cloned.1.call-done = f32[5,128,128]{2,1,0:T(8,128)} async-done(((f32[5,128,128]{2,1,0:T(8,128)}), f32[5,128,128]{2,1,0:T(8,128)}) %all-reduce.11.cloned.1.call-update) | async-done | bytes 327696 | tf_op jit(solution)/shard_map/psum | solution.py:104
  796.5 1.0 broadcast_multiply_fusion.1
  798.2 1.3 copy.137
  799.4 13.5 %all-to-all-start.3 = ((bf16[2,5,128,128]{3,0,1,2:T(2,128)(2,1)}), bf16[2,5,128,128]{3,0,1,2:T(2,128)(2,1)S(1)}, u32[]{:S(2)}, u32[]{:S(2)}) async-start(bf16[2,5,128,128]{3,0,1,2:T(2,128)(2,1)} %copy.137), calls=%async_computation.3 | async-start | bytes 655360 | tf_op jit(solution)/shard_map/all_to_all | solution.py:115
  813.4 0.8 copy.147
  814.2 22.2 %all-to-all-done.3 = bf16[2,5,128,128]{3,0,1,2:T(2,128)(2,1)S(1)} async-done(((bf16[2,5,128,128]{3,0,1,2:T(2,128)(2,1)}), bf16[2,5,128,128]{3,0,1,2:T(2,128)(2,1)S(1)}, u32[]{:S(2)}, u32[]{:S(2)}) %all-to-all-start.3) | async-done | bytes 327712 | tf_op jit(solution)/shard_map/all_to_all | solution.py:115
  837.6 0.8 fusion.64
  843.8 1.0 fusion.34
  (157 shorter events, 63.6 us)
Async XLA Ops:
  7.2 66.3 %copy-start = (bf16[5,128,128]{2,1,0:T(8,128)(2,1)S(1)}, bf16[5,128,128]{2,1,0:T(8,128)(2,1)}, u32[]{:S(2)}) copy-start(bf16[5,128,128]{2,1,0:T(8,128)(2,1)} %param.16) | copy-start | bytes 491524
  8.0 2.8 copy-start.7
  12.5 36.1 %copy-start.9 = (bf16[2,5,128,128]{3,2,1,0:T(8,128)(2,1)S(1)}, bf16[2,5,128,128]{3,2,1,0:T(8,128)(2,1)}, u32[]{:S(2)}) copy-start(bf16[2,5,128,128]{3,2,1,0:T(8,128)(2,1)} %param.13) | copy-start | bytes 983044
  32.4 40.9 %all-to-all-start = ((bf16[32,2,5,4,128]{4,3,2,1,0:T(4,128)(2,1)}), bf16[32,2,5,4,128]{4,3,2,1,0:T(4,128)(2,1)S(1)}, u32[]{:S(2)}, u32[]{:S(2)}) async-start(bf16[32,2,5,4,128]{4,3,2,1,0:T(4,128)(2,1)} %constant_dynamic-update-slice_fusion), calls=%async_computation | async-start | bytes 655360 | tf_op jit(solution)/shard_map/all_to_all | solution.py:86
  48.5 169.7 %all-reduce.5.cloned.1.call-start = ((), (), s32[]{:S(2)}) async-start(), calls=%async_computation.4 | async-start | bytes 655360 | tf_op jit(solution)/shard_map/psum | solution.py:97
  73.3 1.4 copy-start.13
  73.3 1.5 copy-start.1
  73.3 1.5 copy-start.8
  74.7 308.7 %all-reduce.7.cloned.1.call-start = ((), (), s32[]{:S(2)}) async-start(), calls=%async_computation.5 | async-start | bytes 655360 | tf_op jit(solution)/shard_map/psum | solution.py:104
  74.7 150.4 %copy-start.14 = (s32[1024]{0:T(1024)}, s32[1024]{0:T(1024)S(1)}, u32[]{:S(2)}) copy-start(s32[1024]{0:T(1024)S(1)} %get-tuple-element.9) | copy-start | bytes 12292
  218.9 6.2 copy-start.10
  218.9 6.2 copy-start.11
  218.9 6.2 copy-start.12
  231.1 0.7 copy-start.6
  431.8 1.0 copy-start.4
  460.6 26.2 %all-to-all-start.2 = ((bf16[32,2,5,4,128]{4,3,2,1,0:T(4,128)(2,1)}), bf16[32,2,5,4,128]{4,3,2,1,0:T(4,128)(2,1)S(1)}, u32[]{:S(2)}, u32[]{:S(2)}) async-start(bf16[32,2,5,4,128]{4,3,2,1,0:T(4,128)(2,1)} %constant_dynamic-update-slice_fusion.32), calls=%async_computation.2 | async-start | bytes 655360 | tf_op jit(solution)/shard_map/all_to_all | solution.py:86
  464.5 166.8 %all-reduce.9.cloned.1.call-start = ((), (), s32[]{:S(2)}) async-start(), calls=%async_computation.6 | async-start | bytes 655360 | tf_op jit(solution)/shard_map/psum | solution.py:97
  486.8 1.6 copy-start.2
  488.2 308.4 %all-reduce.11.cloned.1.call-start = ((), (), s32[]{:S(2)}) async-start(), calls=%async_computation.7 | async-start | bytes 655360 | tf_op jit(solution)/shard_map/psum | solution.py:104
  644.3 0.7 copy-start.5
  797.7 15.2 %copy-start.3 = (f32[5,128,128]{2,1,0:T(8,128)S(1)}, f32[5,128,128]{2,1,0:T(8,128)}, u32[]{:S(2)}) copy-start(f32[5,128,128]{2,1,0:T(8,128)} %all-reduce.11.cloned.1.call-done) | copy-start | bytes 983044
  799.4 37.0 %all-to-all-start.3 = ((bf16[2,5,128,128]{3,0,1,2:T(2,128)(2,1)}), bf16[2,5,128,128]{3,0,1,2:T(2,128)(2,1)S(1)}, u32[]{:S(2)}, u32[]{:S(2)}) async-start(bf16[2,5,128,128]{3,0,1,2:T(2,128)(2,1)} %copy.137), calls=%async_computation.3 | async-start | bytes 655360 | tf_op jit(solution)/shard_map/all_to_all | solution.py:115
Sparse Core Ops, SparseCore 0:
  74.8 143.3 all-reduce.4
  232.0 151.3 all-reduce.6
  488.3 142.9 all-reduce.8
  645.1 151.3 all-reduce.10
